TPU v7x, 32 devices: a whole 2x2x4 slice. The times are simulated.
32 devices in a mesh: role: 4 (over z), grp: 4 (over x, core), run: 2 (over y).
Axes of the slice: x: 2, y: 2, z: 4, core: 2. Of those that a mesh axis runs over, the one named last changes fastest.
Arguments:
- prior_fields: float32 [1024, 3, 32, 128], P(('role', 'grp'), None, 'run'), may hold values from -0.4 to 1.4, as said below
- measured_point_location: int32 [512], P('run'), may hold values from 0 to 2047
- measured_depths: float32 [512], P('run'), may hold values from 0.7 to 1.3
- inverse_noise_deviation: float32 [512], P('run'), may hold values from 5 to 40
- sample_noise_draw: float32 [1024, 512], P(None, 'run'), may hold values from -6 to 6
- sample_line_labels: int32 [1024], P(('role', 'grp')), may hold values from 0 to 1023, each once
Outputs:
- analysis: float32 [1024, 3, 32, 128], P(('role', 'grp'), None, 'run')
Inputs may be any that keep to these rules, and one draw needn't show every extreme that they name: `prior_fields`: the depth component (index 0 of the second dimension) lies within 0.75 to 1.4, the momenta within -0.4 to 0.4.
All inputs are finite; a program needn't handle non-finite values.
Results may differ from a plain program's by a relative error of at most 0.0003.
Values sent between devices are 32-bit elements; how exact they have to be, the bound alone decides.
A program may use at most 64 MiB of HBM per device.

v0:
```python
import functools
import math

import jax
import jax.numpy as jnp
from jax import lax
from jax.experimental import pallas as pl
from jax.experimental.pallas import tpu as pltpu
from jax.sharding import PartitionSpec as P

STEPS = 4
CHEB = 8
CHUNKS = 4
TILE = 8

gravity = 1.0
courant = 0.35
widen_dispersion = 1.1

MESH = pl.DeviceIdType.MESH


def advance(fields):
    depth, east, north = fields
    half = 0.5 * courant
    inverse = 1.0 / depth
    press = 0.5 * gravity * depth * depth
    speed_x = east * inverse
    speed_y = north * inverse
    mixed = east * speed_y
    flux_x = (east, east * speed_x + press, mixed)
    flux_y = (north, mixed, north * speed_y + press)
    rows = depth.shape[0]
    out = []
    for q, fx, fy in zip(fields, flux_x, flux_y):
        quarter = 0.25 * q
        mid = quarter[1:-1]
        kx = half * fx[1:-1]
        sides = pltpu.roll(mid - kx, q.shape[2] - 1, 2) + pltpu.roll(mid + kx, 1, 2)
        up = (quarter - half * fy)[2:]
        down = (quarter + half * fy)[: rows - 2]
        out.append(sides + up + down)
    return tuple(out)


def halves(value):
    high = value.astype(jnp.bfloat16)
    return high, (value - high.astype(jnp.float32)).astype(jnp.bfloat16)


def dot(left, right, dims=((1,), (0,))):
    return lax.dot_general(left, right, (dims, ((), ())), preferred_element_type=jnp.float32)


def dot3(left, right, dims=((1,), (0,))):
    (lh, ll), (rh, rl) = left, right
    return dot(lh, rh, dims) + (dot(lh, rl, dims) + dot(ll, rh, dims))


def kernel(
    dims,
    x_ref, loc_ref, inv_ref, noise_ref,
    out_ref,
    halo, stepped, everyone, result, sampled, noise,
    st_hi, st_lo, gram_hi, gram_lo, res, direc, poly,
    halo_send, halo_recv, s_send, s_recv, n_send, n_recv, f_send, f_recv, b_send, b_recv,
):
    nz, nx, nc, ny = dims
    z = lax.axis_index("role")
    grp = lax.axis_index("grp")
    y = lax.axis_index("run")
    x = grp // nc
    c = grp % nc
    rows, _, members, cols = x_ref.shape
    obs = loc_ref.shape[1]
    total = nz * nx * nc * members
    width = halo.shape[1]

    def device(zz, xx, cc, yy):
        return (zz, xx * nc + cc, yy)

    def flat(cc, xx, zz):
        return (cc * nx + xx) * nz + zz

    me = flat(c, x, z)
    offsets = [(dz, dx, dc) for dz in range(nz) for dx in range(nx) for dc in range(nc)][1:]
    far = {0: 0, nz // 2: 2}
    offsets.sort(key=lambda o: (-far.get(o[0], 1), -o[1], -o[2]))

    def shifted(off):
        dz, dx, dc = off
        return lax.rem(z + dz, nz), lax.rem(x + dx, nx), lax.rem(c + dc, nc)

    other_y = lax.rem(y + 1, ny)

    barrier = pltpu.get_barrier_semaphore()
    for off in offsets:
        zz, xx, cc = shifted(off)
        pl.semaphore_signal(barrier, inc=1, device_id=device(zz, xx, cc, y), device_id_type=MESH)
    pl.semaphore_signal(barrier, inc=1, device_id=device(z, x, c, other_y), device_id_type=MESH)
    pl.semaphore_wait(barrier, len(offsets) + 1)

    def remote(src, dst, send, recv, target):
        return pltpu.make_async_remote_copy(
            src_ref=src, dst_ref=dst, send_sem=send, recv_sem=recv, device_id=target, device_id_type=MESH
        )

    per = members // CHUNKS
    halo_copies = []
    for k in range(CHUNKS):
        part = pl.ds(k * per, per)
        pair = (
            remote(x_ref.at[pl.ds(rows - width, width), :, part], halo.at[0, :, :, part],
                   halo_send.at[2 * k], halo_recv.at[2 * k], device(z, x, c, other_y)),
            remote(x_ref.at[pl.ds(0, width), :, part], halo.at[1, :, :, part],
                   halo_send.at[2 * k + 1], halo_recv.at[2 * k + 1], device(z, x, c, other_y)),
        )
        for copy in pair:
            copy.start()
        halo_copies.append(pair)

    def along_z(buf, send, recv):
        return [
            remote(buf.at[c, y, x, z], buf.at[c, y, x, z], send.at[d - 1], recv.at[d - 1],
                   device(lax.rem(z + d, nz), x, c, y))
            for d in range(1, nz)
        ]

    def along_x(buf, send, recv):
        return remote(buf.at[c, y, x], buf.at[c, y, x], send.at[nz], recv.at[nz],
                      device(z, lax.rem(x + 1, nx), c, y))

    def along_y(buf, send, recv):
        return remote(buf.at[c, y], buf.at[c, y], send.at[nz + 1], recv.at[nz + 1],
                      device(z, x, c, other_y))

    def along_core(buf, send, recv):
        return remote(buf.at[c], buf.at[c], send.at[nz + 2], recv.at[nz + 2],
                      device(z, x, lax.rem(c + 1, nc), y))

    noise[c, y, x, z] = noise_ref[...]
    noise_z = along_z(noise, n_send, n_recv)
    for copy in noise_z:
        copy.start()

    for k in range(CHUNKS):
        for copy in halo_copies[k]:
            copy.wait()

        def tile(t, carry):
            at = pl.ds(pl.multiple_of(k * per + t * TILE, TILE), TILE)
            fields = tuple(
                jnp.concatenate([halo[0, :, f, at], x_ref[:, f, at], halo[1, :, f, at]], 0) for f in range(3)
            )
            for step in range(STEPS):
                fields = advance(fields)
            for f in range(3):
                stepped[:, f, at] = fields[f]
            return carry

        lax.fori_loop(0, per // TILE, tile, 0)

    loc = loc_ref[...]
    lanes = lax.broadcasted_iota(jnp.int32, (cols, obs), 0)

    def pick(r, acc):
        hot = jnp.where(loc - r * cols == lanes, 1.0, 0.0).astype(jnp.bfloat16)
        depth = stepped[r, 0]
        d1 = depth.astype(jnp.bfloat16)
        rest = depth - d1.astype(jnp.float32)
        d2 = rest.astype(jnp.bfloat16)
        d3 = (rest - d2.astype(jnp.float32)).astype(jnp.bfloat16)
        return acc + (dot(d1, hot) + (dot(d2, hot) + dot(d3, hot)))

    own_sampled = inv_ref[...] * lax.fori_loop(0, rows, pick, jnp.zeros((members, obs), jnp.float32))
    sampled[c, y, x, z] = own_sampled
    s_z = along_z(sampled, s_send, s_recv)
    for copy in s_z:
        copy.start()

    forward = {}
    for i, off in enumerate(offsets):
        zz, xx, cc = shifted(off)
        forward[off] = remote(stepped.at[flat(cc, xx, zz)], everyone.at[me], f_send.at[i], f_recv.at[i],
                              device(zz, xx, cc, y))
    for off in offsets:
        if off[1] == 0:
            forward[off].start()
    everyone[me] = stepped[me]

    for copy in s_z:
        copy.wait()
    s_x = along_x(sampled, s_send, s_recv)
    s_x.start()
    for off in offsets:
        if off[1] != 0:
            forward[off].start()
    for copy in noise_z:
        copy.wait()
    n_x = along_x(noise, n_send, n_recv)
    n_x.start()
    s_x.wait()
    s_y = along_y(sampled, s_send, s_recv)
    s_y.start()
    n_x.wait()
    n_y = along_y(noise, n_send, n_recv)
    n_y.start()
    s_y.wait()
    s_c = along_core(sampled, s_send, s_recv)
    s_c.start()
    s_c.wait()

    dispersion = math.sqrt(widen_dispersion / (total - 1))
    for yy in range(ny):
        block = sampled[:, yy].reshape(total, obs)
        spread = dispersion * (block - jnp.sum(block, axis=0, keepdims=True) * (1.0 / total))
        hi, lo = halves(spread.T)
        st_hi[pl.ds(yy * obs, obs)] = hi
        st_lo[pl.ds(yy * obs, obs)] = lo

    nt = ((1,), (1,))
    every = ny * obs
    sth = st_hi[...]
    stl = st_lo[...]
    gram = dot3((sth, stl), (sth, stl), nt)
    ghi, glo = halves(gram)
    gram_hi[...] = ghi
    gram_lo[...] = glo
    upper = 1.0 + jnp.sqrt(jnp.sum(jnp.sum(gram * gram, axis=1, keepdims=True), axis=0, keepdims=True))
    theta = (upper + 1.0) / 2.0
    delta = (upper - 1.0) / 2.0
    sigma = theta / delta
    eye = jnp.where(
        lax.broadcasted_iota(jnp.int32, (every, every), 0) == lax.broadcasted_iota(jnp.int32, (every, every), 1),
        1.0, 0.0,
    )
    res[...] = eye
    start = eye * (1.0 / theta)
    direc[...] = start
    poly[...] = start

    n_y.wait()
    n_c = along_core(noise, n_send, n_recv)
    n_c.start()

    def turn(i, rho):
        d = direc[...]
        prod = dot3(halves(d), (gram_hi[...], gram_lo[...]))
        r = res[...] - d - prod
        res[...] = r
        rho_next = 1.0 / (2.0 * sigma - rho)
        d = (rho_next * rho) * d + (2.0 * rho_next / delta) * r
        direc[...] = d
        poly[...] = poly[...] + d
        return rho_next

    lax.fori_loop(0, CHEB - 1, turn, 1.0 / sigma)

    for off in offsets:
        forward[off].wait()
    n_c.wait()

    center = []
    devs = []
    for f in range(3):
        values = everyone[:, f].reshape(total, cols)
        mean = jnp.sum(values, axis=0, keepdims=True) * (1.0 / total)
        center.append(mean)
        devs.append(values - mean)
    dev = jnp.concatenate(devs, 1)
    cross = dot3((st_hi[...], st_lo[...]), halves(dev))
    weights = dispersion * dot3(halves(poly[...]), halves(cross))
    whi, wlo = halves(weights)

    def analyse(cc, xx, zz):
        at = flat(cc, xx, zz)
        innov = jnp.concatenate(
            [
                noise[cc, yy, xx, zz] - sampled[cc, yy, xx, zz]
                for yy in range(ny)
            ],
            1,
        )
        gain = dot3(halves(innov), (whi, wlo))
        for f in range(3):
            result[at, f] = (
                center[f]
                + math.sqrt(widen_dispersion) * (everyone[at, f] - center[f])
                + gain[:, f * cols : (f + 1) * cols]
            )
        return at

    back = []
    for i, off in enumerate(offsets):
        zz, xx, cc = shifted(off)
        at = analyse(cc, xx, zz)
        copy = remote(result.at[at], out_ref.at[me], b_send.at[i], b_recv.at[i], device(zz, xx, cc, y))
        copy.start()
        back.append(copy)
    at = analyse(c, x, z)
    out_ref[me] = result[at]
    for copy in back:
        copy.wait()


def with_halo(cells, sides, width):
    for axis, dim in sides:
        count = lax.axis_size(axis)
        head = lax.slice_in_dim(cells, 0, width, axis=dim)
        tail = lax.slice_in_dim(cells, cells.shape[dim] - width, cells.shape[dim], axis=dim)
        cells = jnp.concatenate(
            [
                lax.ppermute(tail, axis, [(i, (i + 1) % count) for i in range(count)]),
                cells,
                lax.ppermute(head, axis, [((i + 1) % count, i) for i in range(count)]),
            ],
            axis=dim,
        )
    return cells


def lax_friedrichs(state):
    depth = state[:, 0]
    east = state[:, 1]
    north = state[:, 2]
    press = 0.5 * gravity * depth * depth
    flux_x = jnp.stack([east, east * east / depth + press, east * north / depth], 1)
    flux_y = jnp.stack([north, east * north / depth, north * north / depth + press], 1)
    inner = state[:, :, 1:-1]
    average = 0.25 * (
        state[:, :, 2:] + state[:, :, :-2] + jnp.roll(inner, 1, 3) + jnp.roll(inner, -1, 3)
    )
    middle = flux_x[:, :, 1:-1]
    return (
        average
        - 0.5 * courant * (jnp.roll(middle, -1, 3) - jnp.roll(middle, 1, 3))
        - 0.5 * courant * (flux_y[:, :, 2:] - flux_y[:, :, :-2])
    )


def product(left, right):
    return jnp.dot(left, right, precision=lax.Precision.HIGHEST, preferred_element_type=jnp.float32)


def plain(
    prior_fields,
    measured_point_location,
    measured_depths,
    inverse_noise_deviation,
    sample_noise_draw,
    sample_line_labels,
):
    dispersion_multiplier = math.sqrt(widen_dispersion / (sample_noise_draw.shape[0] - 1))
    propagated_fields = prior_fields
    for step in range(STEPS):
        padded = with_halo(propagated_fields, (("run", 2),), 1)
        propagated_fields = lax_friedrichs(padded)
    members = propagated_fields.shape[0]
    depth_flat = propagated_fields[:, 0].reshape(
        members, propagated_fields.shape[2] * propagated_fields.shape[3]
    )
    sampled = inverse_noise_deviation[None, :] * jnp.take(
        depth_flat, measured_point_location, axis=1
    )
    innovation = (
        inverse_noise_deviation[None, :] * measured_depths[None, :]
        - sampled
        + jnp.take(sample_noise_draw, sample_line_labels, axis=0)
    )
    all_sampled, all_innov = (
        lax.all_gather(sampled, ("role", "grp"), axis=0, tiled=True),
        lax.all_gather(innovation, ("role", "grp"), axis=0, tiled=True),
    )
    spread = dispersion_multiplier * (all_sampled - jnp.mean(all_sampled, axis=0, keepdims=True))
    first = lax.axis_index(("role", "grp")) * members
    own_spread = lax.dynamic_slice_in_dim(spread, first, members, 0)
    own_innov = lax.dynamic_slice_in_dim(all_innov, first, members, 0)
    gram_rows, cross_rows = (
        lax.psum_scatter(product(own_spread, spread.T), "run", scatter_dimension=0, tiled=True),
        lax.psum_scatter(product(own_innov, spread.T), "run", scatter_dimension=0, tiled=True),
    )
    gram = lax.all_gather(gram_rows, ("role", "grp", "run"), axis=0, tiled=True)
    upper = 1.0 + jnp.sqrt(jnp.sum(gram * gram))
    theta = (upper + 1.0) / 2.0
    delta = (upper - 1.0) / 2.0
    sigma = theta / delta
    rho = 1.0 / sigma
    residual = cross_rows
    direction = residual / theta
    linear_solution = direction
    for turn in range(CHEB - 1):
        residual = residual - direction - product(direction, gram)
        rho_next = 1.0 / (2.0 * sigma - rho)
        direction = rho_next * rho * direction + 2.0 * rho_next / delta * residual
        linear_solution = linear_solution + direction
        rho = rho_next
    posterior_coefficients = lax.all_gather(
        linear_solution, ("role", "grp", "run"), axis=0, tiled=True
    )
    ensemble_combination = (
        math.sqrt(widen_dispersion) * jnp.eye(posterior_coefficients.shape[0], dtype=jnp.float32)
        + dispersion_multiplier * posterior_coefficients
    )
    strip_slab = lax.all_to_all(
        propagated_fields, ("role", "grp"), split_axis=2, concat_axis=0, tiled=True
    )
    array_shape = strip_slab.shape
    flat = strip_slab.reshape(array_shape[0], array_shape[1] * array_shape[2] * array_shape[3])
    center = jnp.mean(flat, axis=0, keepdims=True)
    updated = (center + product(ensemble_combination, flat - center)).reshape(array_shape)
    return lax.all_to_all(updated, ("role", "grp"), split_axis=0, concat_axis=2, tiled=True)


def fused(
    dims,
    prior_fields,
    measured_point_location,
    measured_depths,
    inverse_noise_deviation,
    sample_noise_draw,
    sample_line_labels,
):
    nz, nx, nc, ny = dims
    members, _, rows, cols = prior_fields.shape
    obs = measured_point_location.shape[0]
    every = ny * obs
    group = nz * nx * nc
    slab = (group, 3, members, cols)
    target = inverse_noise_deviation[None, :] * measured_depths[None, :] + jnp.take(
        sample_noise_draw, sample_line_labels, axis=0
    )
    gathered = (nc, ny, nx, nz, members, obs)
    dma = pltpu.SemaphoreType.DMA
    out = pl.pallas_call(
        functools.partial(kernel, dims),
        out_shape=jax.ShapeDtypeStruct(slab, jnp.float32),
        in_specs=[pl.BlockSpec(memory_space=pltpu.VMEM)] * 4,
        out_specs=pl.BlockSpec(memory_space=pltpu.VMEM),
        scratch_shapes=[
            pltpu.VMEM((2, STEPS, 3, members, cols), jnp.float32),
            pltpu.VMEM(slab, jnp.float32),
            pltpu.VMEM(slab, jnp.float32),
            pltpu.VMEM(slab, jnp.float32),
            pltpu.VMEM(gathered, jnp.float32),
            pltpu.VMEM(gathered, jnp.float32),
            pltpu.VMEM((every, group * members), jnp.bfloat16),
            pltpu.VMEM((every, group * members), jnp.bfloat16),
            pltpu.VMEM((every, every), jnp.bfloat16),
            pltpu.VMEM((every, every), jnp.bfloat16),
            pltpu.VMEM((every, every), jnp.float32),
            pltpu.VMEM((every, every), jnp.float32),
            pltpu.VMEM((every, every), jnp.float32),
            dma((2 * CHUNKS,)),
            dma((2 * CHUNKS,)),
            dma((nz + 3,)),
            dma((nz + 3,)),
            dma((nz + 3,)),
            dma((nz + 3,)),
            dma((group,)),
            dma((group,)),
            dma((group,)),
            dma((group,)),
        ],
        compiler_params=pltpu.CompilerParams(
            collective_id=0, has_side_effects=True, vmem_limit_bytes=60 * 1024 * 1024
        ),
        name="analysis_kernel",
    )(
        prior_fields.transpose(2, 1, 0, 3),
        measured_point_location[None, :],
        inverse_noise_deviation[None, :],
        target,
    )
    return out.transpose(2, 1, 0, 3)


def shards(shape, *args):
    nz, grp, ny = shape["role"], shape["grp"], shape["run"]
    members, _, rows, cols = args[0].shape
    fits = (
        grp == 4
        and ny == 2
        and rows == nz * grp
        and members % (CHUNKS * TILE) == 0
        and cols == 128
        and args[1].shape[0] * ny <= 512
    )
    if fits:
        return fused((nz, 2, 2, ny), *args)
    return plain(*args)


def solution(mesh):
    placed = (
        P(("role", "grp"), None, "run", None),
        P("run"),
        P("run"),
        P("run"),
        P(None, "run"),
        P(("role", "grp")),
    )
    return jax.shard_map(
        functools.partial(shards, dict(mesh.shape)),
        mesh=mesh,
        in_specs=placed,
        out_specs=P(("role", "grp"), None, "run", None),
        check_vma=False,
    )
```

profile of v0, /device:TPU:13, one launch (start us, length us, event | category | flops | bytes accessed | tf_op | source)
XLA Modules:
  0.0 128.9 jit_solution(6763343837493383937)
XLA Ops:
  0.0 0.0 copy-start
  0.0 0.8 compare_and_fusion
  0.8 0.7 compare_select_fusion
  1.4 0.7 mul.4
  2.1 0.0 copy-done
  2.1 0.7 gather_fusion
  2.8 0.7 select_add_fusion.noise_ref
  3.5 3.1 %copy.10 = f32[64,3,16,128]{3,0,1,2:T(8,128)} copy(f32[64,3,16,128]{3,2,1,0:T(8,128)} %param.6) | data formatting | bytes 3145728 | tf_op args[0]
  6.5 118.9 %analysis_kernel.1 = f32[16,3,64,128]{3,2,1,0:T(8,128)} custom-call(f32[16,3,64,128]{3,2,1,0:T(8,128)} %bitcast.7, s32[1,256]{1,0:T(1,128)} %bitcast.9, f32[1,256]{1,0:T(1,128)} %bitcast.8, f32[64,256]{1,0:T(8,128)} %select_add_fusion.noise_ref), custom_call_target="tpu_custom_call" | custom-call | tf_op jit(solution)/shard_map/analysis_kernel/pallas_call | solution.py:434
  125.4 3.5 %copy.8 = f32[64,3,16,128]{3,2,1,0:T(8,128)} copy(f32[64,3,16,128]{3,0,1,2:T(8,128)} %bitcast.6) | data formatting | bytes 3145728 | tf_op jit(solution)/shard_map/transpose | solution.py:474
  (1 shorter events, 0.0 us)
Async XLA Ops:
  0.0 2.1 %copy-start = (f32[1024,256]{1,0:T(8,128)S(1)}, f32[1024,256]{1,0:T(8,128)}, u32[]{:S(2)}) copy-start(f32[1024,256]{1,0:T(8,128)} %param.10) | copy-start | bytes 3145732
where the time goes:
time: 131 us; the launch traced here: 129 us
  Pallas kernels  119 us (91%)
  local copies, waits for them, and re-layouts  7.18 us (5%)
  other arithmetic  2.81 us (2%)
    pallas_call x1, Pallas kernels, fused(): pl.pallas_call(functools.partial(kernel, dims), out_shape=jax.ShapeDtypeS...  119 us
    transpose x1, local copies, waits for them, and re-layouts, fused(): return out.transpose(2, 1, 0, 3)  3.46 us
    unnamed x3, local copies, waits for them, and re-layouts  3.06 us

commit v1 on v0

--- a/solution.py
+++ b/solution.py
@@ -59,9 +59,9 @@
 
 def kernel(
     dims,
-    x_ref, loc_ref, inv_ref, noise_ref,
+    label_ref, x_ref, loc_ref, inv_ref, meas_ref, table_ref,
     out_ref,
-    halo, stepped, everyone, result, sampled, noise,
+    halo, stepped, everyone, result, sampled, noise, hot,
     st_hi, st_lo, gram_hi, gram_lo, res, direc, poly,
     halo_send, halo_recv, s_send, s_recv, n_send, n_recv, f_send, f_recv, b_send, b_recv,
 ):
@@ -85,7 +85,7 @@
     me = flat(c, x, z)
     offsets = [(dz, dx, dc) for dz in range(nz) for dx in range(nx) for dc in range(nc)][1:]
     far = {0: 0, nz // 2: 2}
-    offsets.sort(key=lambda o: (-far.get(o[0], 1), -o[1], -o[2]))
+    offsets.sort(key=lambda o: (-far.get(o[0], 1), o[0], -o[1], -o[2]))
 
     def shifted(off):
         dz, dx, dc = off
@@ -119,30 +119,83 @@
             copy.start()
         halo_copies.append(pair)
 
-    def along_z(buf, send, recv):
-        return [
-            remote(buf.at[c, y, x, z], buf.at[c, y, x, z], send.at[d - 1], recv.at[d - 1],
-                   device(lax.rem(z + d, nz), x, c, y))
-            for d in range(1, nz)
-        ]
-
-    def along_x(buf, send, recv):
-        return remote(buf.at[c, y, x], buf.at[c, y, x], send.at[nz], recv.at[nz],
-                      device(z, lax.rem(x + 1, nx), c, y))
-
-    def along_y(buf, send, recv):
-        return remote(buf.at[c, y], buf.at[c, y], send.at[nz + 1], recv.at[nz + 1],
-                      device(z, x, c, other_y))
-
-    def along_core(buf, send, recv):
-        return remote(buf.at[c], buf.at[c], send.at[nz + 2], recv.at[nz + 2],
-                      device(z, x, lax.rem(c + 1, nc), y))
-
-    noise[c, y, x, z] = noise_ref[...]
-    noise_z = along_z(noise, n_send, n_recv)
-    for copy in noise_z:
-        copy.start()
-
+    xo = lax.rem(x + 1, nx)
+    co = lax.rem(c + 1, nc)
+    east_side = device(z, xo, c, y)
+    north_side = device(z, x, c, other_y)
+    twin = device(z, x, co, y)
+    hops = nz - 1
+
+    class Gather:
+        def __init__(self, buf, send, recv, base, part):
+            self.buf, self.send, self.recv, self.base, self.part = buf, send, recv, base, part
+            self.open = {}
+
+        def go(self, name, slot, line, one, target):
+            yy, xx = line
+            where = (c, yy, xx, z, self.part) if one else (c, yy, xx, slice(None), self.part)
+            piece = self.buf.at[where]
+            copy = remote(piece, piece, self.send.at[self.base + slot], self.recv.at[self.base + slot], target)
+            copy.start()
+            self.open[name] = copy
+
+        def take(self, name):
+            self.open.pop(name).wait()
+
+        def first(self):
+            for d in range(1, nz):
+                self.go(("z", d), d - 1, (y, x), True, device(lax.rem(z + d, nz), x, c, y))
+
+        def spread(self, north=True):
+            for d in range(1, nz):
+                self.take(("z", d))
+            if north:
+                self.north()
+            self.go("x", hops + 1, (y, x), False, east_side)
+            self.go("c0", hops + 3, (y, x), False, twin)
+
+        def north(self):
+            self.go("y", hops, (y, x), False, north_side)
+
+        def relay_east(self):
+            self.take("x")
+            self.go("c1", hops + 4, (y, xo), False, twin)
+
+        def relay_north(self):
+            self.take("y")
+            self.go("xo", hops + 2, (other_y, x), False, east_side)
+            self.go("c2", hops + 5, (other_y, x), False, twin)
+
+        def relay_last(self):
+            self.take("xo")
+            self.go("c3", hops + 6, (other_y, xo), False, twin)
+
+        def finish(self):
+            for name in list(self.open):
+                self.take(name)
+
+    def fetch(i, carry):
+        noise[c, y, x, z, pl.ds(i, 1)] = table_ref[pl.ds(label_ref[i], 1)]
+        return carry
+
+    lax.fori_loop(0, members, fetch, 0)
+    noise[c, y, x, z] = noise[c, y, x, z] + inv_ref[...] * meas_ref[...]
+    noise_gather = Gather(noise, n_send, n_recv, 0, slice(None))
+    noise_gather.first()
+
+    loc = loc_ref[...]
+    lanes = lax.broadcasted_iota(jnp.int32, (cols, obs), 0)
+
+    def mark(r, carry):
+        at = pl.ds(pl.multiple_of(r * cols, cols), cols)
+        hot[at] = jnp.where(loc - r * cols == lanes, 1.0, 0.0).astype(jnp.bfloat16)
+        return carry
+
+    lax.fori_loop(0, rows, mark, 0)
+    noise_gather.spread(north=False)
+
+    gathers = []
+    forward = []
     for k in range(CHUNKS):
         for copy in halo_copies[k]:
             copy.wait()
@@ -160,55 +213,39 @@
 
         lax.fori_loop(0, per // TILE, tile, 0)
 
-    loc = loc_ref[...]
-    lanes = lax.broadcasted_iota(jnp.int32, (cols, obs), 0)
-
-    def pick(r, acc):
-        hot = jnp.where(loc - r * cols == lanes, 1.0, 0.0).astype(jnp.bfloat16)
-        depth = stepped[r, 0]
+        part = pl.ds(k * per, per)
+        depth = jnp.concatenate([stepped[r, 0, part] for r in range(rows)], 1)
         d1 = depth.astype(jnp.bfloat16)
         rest = depth - d1.astype(jnp.float32)
         d2 = rest.astype(jnp.bfloat16)
         d3 = (rest - d2.astype(jnp.float32)).astype(jnp.bfloat16)
-        return acc + (dot(d1, hot) + (dot(d2, hot) + dot(d3, hot)))
-
-    own_sampled = inv_ref[...] * lax.fori_loop(0, rows, pick, jnp.zeros((members, obs), jnp.float32))
-    sampled[c, y, x, z] = own_sampled
-    s_z = along_z(sampled, s_send, s_recv)
-    for copy in s_z:
-        copy.start()
-
-    forward = {}
-    for i, off in enumerate(offsets):
-        zz, xx, cc = shifted(off)
-        forward[off] = remote(stepped.at[flat(cc, xx, zz)], everyone.at[me], f_send.at[i], f_recv.at[i],
-                              device(zz, xx, cc, y))
-    for off in offsets:
-        if off[1] == 0:
-            forward[off].start()
+        found = dot(jnp.concatenate([d1, d2, d3], 0), hot[...])
+        found = found[:per] + (found[per : 2 * per] + found[2 * per :])
+        sampled[c, y, x, z, part] = inv_ref[...] * found
+        gather = Gather(sampled, s_send, s_recv, k * (hops + 7), part)
+        gather.first()
+        gathers.append(gather)
+        if k > 0:
+            gathers[k - 1].spread()
+        for i, off in enumerate(offsets):
+            zz, xx, cc = shifted(off)
+            copy = remote(stepped.at[flat(cc, xx, zz), :, part], everyone.at[me, :, part],
+                          f_send.at[k * len(offsets) + i], f_recv.at[k * len(offsets) + i], device(zz, xx, cc, y))
+            copy.start()
+            forward.append(copy)
+
+    gathers[-1].spread()
     everyone[me] = stepped[me]
-
-    for copy in s_z:
-        copy.wait()
-    s_x = along_x(sampled, s_send, s_recv)
-    s_x.start()
-    for off in offsets:
-        if off[1] != 0:
-            forward[off].start()
-    for copy in noise_z:
-        copy.wait()
-    n_x = along_x(noise, n_send, n_recv)
-    n_x.start()
-    s_x.wait()
-    s_y = along_y(sampled, s_send, s_recv)
-    s_y.start()
-    n_x.wait()
-    n_y = along_y(noise, n_send, n_recv)
-    n_y.start()
-    s_y.wait()
-    s_c = along_core(sampled, s_send, s_recv)
-    s_c.start()
-    s_c.wait()
+    for gather in gathers:
+        gather.relay_north()
+    for gather in gathers:
+        gather.relay_east()
+    noise_gather.north()
+    noise_gather.relay_east()
+    for gather in gathers:
+        gather.relay_last()
+    for gather in gathers:
+        gather.finish()
 
     dispersion = math.sqrt(widen_dispersion / (total - 1))
     for yy in range(ny):
@@ -239,9 +276,7 @@
     direc[...] = start
     poly[...] = start
 
-    n_y.wait()
-    n_c = along_core(noise, n_send, n_recv)
-    n_c.start()
+    noise_gather.relay_north()
 
     def turn(i, rho):
         d = direc[...]
@@ -256,9 +291,10 @@
 
     lax.fori_loop(0, CHEB - 1, turn, 1.0 / sigma)
 
-    for off in offsets:
-        forward[off].wait()
-    n_c.wait()
+    noise_gather.relay_last()
+    for copy in forward:
+        copy.wait()
+    noise_gather.finish()
 
     center = []
     devs = []
@@ -272,33 +308,42 @@
     weights = dispersion * dot3(halves(poly[...]), halves(cross))
     whi, wlo = halves(weights)
 
-    def analyse(cc, xx, zz):
-        at = flat(cc, xx, zz)
+    def analyse(places):
         innov = jnp.concatenate(
             [
-                noise[cc, yy, xx, zz] - sampled[cc, yy, xx, zz]
-                for yy in range(ny)
+                jnp.concatenate([noise[cc, yy, xx, zz] - sampled[cc, yy, xx, zz] for yy in range(ny)], 1)
+                for zz, xx, cc in places
             ],
-            1,
+            0,
         )
-        gain = dot3(halves(innov), (whi, wlo))
-        for f in range(3):
-            result[at, f] = (
-                center[f]
-                + math.sqrt(widen_dispersion) * (everyone[at, f] - center[f])
-                + gain[:, f * cols : (f + 1) * cols]
-            )
-        return at
+        high, low = halves(innov)
+        count = innov.shape[0]
+        both = dot(jnp.concatenate([high, low], 0), whi)
+        gain = both[:count] + (both[count:] + dot(high, wlo))
+        for n, (zz, xx, cc) in enumerate(places):
+            at = flat(cc, xx, zz)
+            for f in range(3):
+                result[at, f] = (
+                    center[f]
+                    + math.sqrt(widen_dispersion) * (everyone[at, f] - center[f])
+                    + gain[n * members : (n + 1) * members, f * cols : (f + 1) * cols]
+                )
 
     back = []
-    for i, off in enumerate(offsets):
-        zz, xx, cc = shifted(off)
-        at = analyse(cc, xx, zz)
-        copy = remote(result.at[at], out_ref.at[me], b_send.at[i], b_recv.at[i], device(zz, xx, cc, y))
-        copy.start()
-        back.append(copy)
-    at = analyse(c, x, z)
-    out_ref[me] = result[at]
+    order = offsets + [(0, 0, 0)]
+    batch = nx * nc
+    for b in range(0, len(order), batch):
+        some = order[b : b + batch]
+        analyse([shifted(off) for off in some])
+        for n, off in enumerate(some):
+            if off == (0, 0, 0):
+                continue
+            zz, xx, cc = shifted(off)
+            copy = remote(result.at[flat(cc, xx, zz)], out_ref.at[me], b_send.at[b + n], b_recv.at[b + n],
+                          device(zz, xx, cc, y))
+            copy.start()
+            back.append(copy)
+    out_ref[me] = result[me]
     for copy in back:
         copy.wait()
 
@@ -426,15 +471,12 @@
     every = ny * obs
     group = nz * nx * nc
     slab = (group, 3, members, cols)
-    target = inverse_noise_deviation[None, :] * measured_depths[None, :] + jnp.take(
-        sample_noise_draw, sample_line_labels, axis=0
-    )
     gathered = (nc, ny, nx, nz, members, obs)
     dma = pltpu.SemaphoreType.DMA
     out = pl.pallas_call(
         functools.partial(kernel, dims),
         out_shape=jax.ShapeDtypeStruct(slab, jnp.float32),
-        in_specs=[pl.BlockSpec(memory_space=pltpu.VMEM)] * 4,
+        in_specs=[pl.BlockSpec(memory_space=pltpu.SMEM)] + [pl.BlockSpec(memory_space=pltpu.VMEM)] * 5,
         out_specs=pl.BlockSpec(memory_space=pltpu.VMEM),
         scratch_shapes=[
             pltpu.VMEM((2, STEPS, 3, members, cols), jnp.float32),
@@ -443,6 +485,7 @@
             pltpu.VMEM(slab, jnp.float32),
             pltpu.VMEM(gathered, jnp.float32),
             pltpu.VMEM(gathered, jnp.float32),
+            pltpu.VMEM((rows * cols, obs), jnp.bfloat16),
             pltpu.VMEM((every, group * members), jnp.bfloat16),
             pltpu.VMEM((every, group * members), jnp.bfloat16),
             pltpu.VMEM((every, every), jnp.bfloat16),
@@ -452,12 +495,12 @@
             pltpu.VMEM((every, every), jnp.float32),
             dma((2 * CHUNKS,)),
             dma((2 * CHUNKS,)),
-            dma((nz + 3,)),
-            dma((nz + 3,)),
-            dma((nz + 3,)),
-            dma((nz + 3,)),
-            dma((group,)),
-            dma((group,)),
+            dma((CHUNKS * (nz + 6),)),
+            dma((CHUNKS * (nz + 6),)),
+            dma((nz + 6,)),
+            dma((nz + 6,)),
+            dma((CHUNKS * group,)),
+            dma((CHUNKS * group,)),
             dma((group,)),
             dma((group,)),
         ],
@@ -466,10 +509,12 @@
         ),
         name="analysis_kernel",
     )(
+        sample_line_labels,
         prior_fields.transpose(2, 1, 0, 3),
         measured_point_location[None, :],
         inverse_noise_deviation[None, :],
-        target,
+        measured_depths[None, :],
+        sample_noise_draw,
     )
     return out.transpose(2, 1, 0, 3)
 

time: 131 us -> 123 us (0.939); the launches traced: 129 us -> 123 us
  other arithmetic: 2.81 us -> 0 us
  Pallas kernels: 119 us -> 117 us
    pallas_call x1, Pallas kernels: 119 us -> 117 us  [fused(): pl.pallas_call(functools.partial(kernel, dims), out_shape=jax.ShapeDtypeS...]
    unnamed x3 -> x1, local copies, waits for them, and re-layouts: 3.06 us -> 3.06 us
where the time goes in v1:
time: 123 us
  Pallas kernels  117 us (95%)
  local copies, waits for them, and re-layouts  6.52 us (5%)
    pallas_call x1, Pallas kernels, fused(): pl.pallas_call(functools.partial(kernel, dims), out_shape=jax.ShapeDtypeS...  117 us
    transpose x1, local copies, waits for them, and re-layouts, fused(): return out.transpose(2, 1, 0, 3)  3.46 us
    unnamed x1, local copies, waits for them, and re-layouts  3.06 us

profile of v1, /device:TPU:13, one launch (start us, length us, event | category | flops | bytes accessed | tf_op | source)
XLA Modules:
  0.0 123.1 jit_solution(11135323676698331834)
XLA Ops:
  0.0 3.1 %copy.10 = f32[64,3,16,128]{3,0,1,2:T(8,128)} copy(f32[64,3,16,128]{3,2,1,0:T(8,128)} %param.6) | data formatting | bytes 3145728 | tf_op args[0]
  3.1 116.6 %analysis_kernel.1 = f32[16,3,64,128]{3,2,1,0:T(8,128)} custom-call(s32[64]{0:T(128)} %label_ref.1, f32[16,3,64,128]{3,2,1,0:T(8,128)} %bitcast.8, s32[1,256]{1,0:T(1,128)} %bitcast.9, f32[1,256]{1,0:T(1,128)} %bitcast.10, f32[1,256]{1,0:T(1,128)} %bitcast.11, f32[1024,256]{1,0:T(8,128)} %table_ref.1), custom_call_target="tpu_custom_call" | custom-call | tf_op jit(solution)/shard_map/analysis_kernel/pallas_call | solution.py:476
  119.7 3.5 %copy.8 = f32[64,3,16,128]{3,2,1,0:T(8,128)} copy(f32[64,3,16,128]{3,0,1,2:T(8,128)} %bitcast.7) | data formatting | bytes 3145728 | tf_op jit(solution)/shard_map/transpose | solution.py:519

commit v2 on v1

--- a/solution.py
+++ b/solution.py
@@ -196,6 +196,24 @@
 
     gathers = []
     forward = []
+    early = (0, nz // 2)
+
+    def ship(off, part, slot):
+        zz, xx, cc = shifted(off)
+        copy = remote(stepped.at[flat(cc, xx, zz), :, part], everyone.at[me, :, part],
+                      f_send.at[slot], f_recv.at[slot], device(zz, xx, cc, y))
+        copy.start()
+        forward.append(copy)
+
+    def ship_early(k, part):
+        for i, off in enumerate(offsets):
+            if off[0] in early:
+                ship(off, part, k * len(offsets) + i)
+
+    def ship_late(dx):
+        for i, off in enumerate(offsets):
+            if off[0] not in early and off[1] == dx:
+                ship(off, slice(None), i)
     for k in range(CHUNKS):
         for copy in halo_copies[k]:
             copy.wait()
@@ -227,17 +245,16 @@
         gathers.append(gather)
         if k > 0:
             gathers[k - 1].spread()
-        for i, off in enumerate(offsets):
-            zz, xx, cc = shifted(off)
-            copy = remote(stepped.at[flat(cc, xx, zz), :, part], everyone.at[me, :, part],
-                          f_send.at[k * len(offsets) + i], f_recv.at[k * len(offsets) + i], device(zz, xx, cc, y))
-            copy.start()
-            forward.append(copy)
+        if k < CHUNKS - 1:
+            ship_early(k, part)
 
     gathers[-1].spread()
+    ship_early(CHUNKS - 1, pl.ds((CHUNKS - 1) * per, per))
+    ship_late(0)
     everyone[me] = stepped[me]
     for gather in gathers:
         gather.relay_north()
+    ship_late(1)
     for gather in gathers:
         gather.relay_east()
     noise_gather.north()

time: 123 us -> 113 us (0.919)
  Pallas kernels: 117 us -> 106 us
    pallas_call x1, Pallas kernels: 117 us -> 106 us  [fused(): pl.pallas_call(functools.partial(kernel, dims), out_shape=jax.ShapeDtypeS...]
where the time goes in v2:
time: 113 us
  Pallas kernels  106 us (94%)
  local copies, waits for them, and re-layouts  6.52 us (6%)
    pallas_call x1, Pallas kernels, fused(): pl.pallas_call(functools.partial(kernel, dims), out_shape=jax.ShapeDtypeS...  106 us
    transpose x1, local copies, waits for them, and re-layouts, fused(): return out.transpose(2, 1, 0, 3)  3.46 us
    unnamed x1, local copies, waits for them, and re-layouts  3.06 us

profile of v2, /device:TPU:13, one launch (start us, length us, event | category | flops | bytes accessed | tf_op | source)
XLA Modules:
  0.0 112.9 jit_solution(3031418696865427512)
XLA Ops:
  0.0 3.1 %copy.10 = f32[64,3,16,128]{3,0,1,2:T(8,128)} copy(f32[64,3,16,128]{3,2,1,0:T(8,128)} %param.6) | data formatting | bytes 3145728 | tf_op args[0]
  3.1 106.3 %analysis_kernel.1 = f32[16,3,64,128]{3,2,1,0:T(8,128)} custom-call(s32[64]{0:T(128)} %label_ref.1, f32[16,3,64,128]{3,2,1,0:T(8,128)} %bitcast.8, s32[1,256]{1,0:T(1,128)} %bitcast.9, f32[1,256]{1,0:T(1,128)} %bitcast.10, f32[1,256]{1,0:T(1,128)} %bitcast.11, f32[1024,256]{1,0:T(8,128)} %table_ref.1), custom_call_target="tpu_custom_call" | custom-call | tf_op jit(solution)/shard_map/analysis_kernel/pallas_call | solution.py:493
  109.4 3.5 %copy.8 = f32[64,3,16,128]{3,2,1,0:T(8,128)} copy(f32[64,3,16,128]{3,0,1,2:T(8,128)} %bitcast.7) | data formatting | bytes 3145728 | tf_op jit(solution)/shard_map/transpose | solution.py:536

commit v3 on v2

--- a/solution.py
+++ b/solution.py
@@ -192,7 +192,6 @@
         return carry
 
     lax.fori_loop(0, rows, mark, 0)
-    noise_gather.spread(north=False)
 
     gathers = []
     forward = []
@@ -245,6 +244,8 @@
         gathers.append(gather)
         if k > 0:
             gathers[k - 1].spread()
+        else:
+            noise_gather.spread(north=False)
         if k < CHUNKS - 1:
             ship_early(k, part)
 

time: 113 us -> 111 us (0.982)
  Pallas kernels: 106 us -> 104 us
    pallas_call x1, Pallas kernels: 106 us -> 104 us  [fused(): pl.pallas_call(functools.partial(kernel, dims), out_shape=jax.ShapeDtypeS...]
where the time goes in v3:
time: 111 us; the launch traced here: 110 us
  Pallas kernels  104 us (94%)
  local copies, waits for them, and re-layouts  6.52 us (6%)
    pallas_call x1, Pallas kernels, fused(): pl.pallas_call(functools.partial(kernel, dims), out_shape=jax.ShapeDtypeS...  104 us
    transpose x1, local copies, waits for them, and re-layouts, fused(): return out.transpose(2, 1, 0, 3)  3.46 us
    unnamed x1, local copies, waits for them, and re-layouts  3.06 us

profile of v3, /device:TPU:13, one launch (start us, length us, event | category | flops | bytes accessed | tf_op | source)
XLA Modules:
  0.0 110.3 jit_solution(4878102583407666515)
XLA Ops:
  0.0 3.1 %copy.10 = f32[64,3,16,128]{3,0,1,2:T(8,128)} copy(f32[64,3,16,128]{3,2,1,0:T(8,128)} %param.6) | data formatting | bytes 3145728 | tf_op args[0]
  3.1 103.8 %analysis_kernel.1 = f32[16,3,64,128]{3,2,1,0:T(8,128)} custom-call(s32[64]{0:T(128)} %label_ref.1, f32[16,3,64,128]{3,2,1,0:T(8,128)} %bitcast.8, s32[1,256]{1,0:T(1,128)} %bitcast.9, f32[1,256]{1,0:T(1,128)} %bitcast.10, f32[1,256]{1,0:T(1,128)} %bitcast.11, f32[1024,256]{1,0:T(8,128)} %table_ref.1), custom_call_target="tpu_custom_call" | custom-call | tf_op jit(solution)/shard_map/analysis_kernel/pallas_call | solution.py:494
  106.9 3.5 %copy.8 = f32[64,3,16,128]{3,2,1,0:T(8,128)} copy(f32[64,3,16,128]{3,0,1,2:T(8,128)} %bitcast.7) | data formatting | bytes 3145728 | tf_op jit(solution)/shard_map/transpose | solution.py:537
